TPU v7x, 768 devices: a whole 4x8x12 slice. The times are simulated.
768 devices in a mesh: seq: 96 (over x, z, core), head: 8 (over y).
Axes of the slice: x: 4, y: 8, z: 12, core: 2. Of those that a mesh axis runs over, the one named last changes fastest.
Arguments:
- queries: bfloat16 [24576, 2048], P('seq', 'head'), may hold values from -6 to 6
- keys: bfloat16 [24576, 2048], P('seq', 'head'), may hold values from -6 to 6
- values: bfloat16 [24576, 2048], P('seq', 'head'), may hold values from -6 to 6
- out_grad: bfloat16 [24576, 2048], P(('seq', 'head')), may hold values from -6 to 6
Outputs:
- attended: bfloat16 [24576, 2048], P('seq', 'head')
- query_grad: bfloat16 [24576, 2048], P('seq', 'head')
- key_grad: bfloat16 [24576, 2048], P('seq', 'head')
- value_grad: bfloat16 [24576, 2048], P('seq', 'head')
All inputs are finite; a program needn't handle non-finite values.
Results may differ from a plain program's by a relative error of at most 0.0049.
Values may be sent and summed in bfloat16 or wider, within the bound.
A program may use at most 32 MiB of HBM per device.

v0:
```python
import math

import jax
import jax.numpy as jnp
from jax import lax
from jax.sharding import PartitionSpec as P

DH = 64
BLOCK = 256


def passed_along(value, axis, steps):
    count = lax.axis_size(axis)
    initial, last = (max(0, -steps), min(count, count - steps))
    return lax.ppermute(value, axis, [(source, source + steps) for source in range(initial, last)])


def on_device(queries, keys, values, out_grad):
    tok_rows = queries.shape[0]
    head_count = queries.shape[1] // DH
    block_count = tok_rows // BLOCK
    factor = 1.0 / math.sqrt(DH * tok_rows * lax.axis_size("seq"))
    grad_local = lax.all_to_all(out_grad, "head", split_axis=1, concat_axis=0, tiled=True)
    layout = (block_count, BLOCK, head_count, DH)
    q_blocks = queries.reshape(layout)
    k_blocks = keys.reshape(layout)
    v_blocks = values.reshape(layout)
    g_blocks = grad_local.reshape(layout)
    block_state = jnp.einsum(
        "nthd,nthe->nhde", k_blocks, v_blocks, preferred_element_type=jnp.float32
    )
    grad_state = jnp.einsum(
        "nthd,nthe->nhde", q_blocks, g_blocks, preferred_element_type=jnp.float32
    )
    state_dev = jnp.sum(block_state, 0)
    grad_dev = jnp.sum(grad_state, 0)
    forward_sum = state_dev
    backward_sum = grad_dev
    span = 1
    while span < lax.axis_size("seq"):
        forward_sum = forward_sum + passed_along(forward_sum, "seq", span)
        backward_sum = backward_sum + passed_along(backward_sum, "seq", -span)
        span = span * 2
    earlier_sum = forward_sum - state_dev
    later_sum = backward_sum - grad_dev
    prefix_state = (earlier_sum[None] + jnp.cumsum(block_state, 0) - block_state).astype(
        jnp.bfloat16
    )
    suffix_state = (later_sum[None] + jnp.cumsum(grad_state[::-1], 0)[::-1] - grad_state).astype(
        jnp.bfloat16
    )
    causal = jnp.arange(BLOCK)[:, None] >= jnp.arange(BLOCK)[None, :]
    scores = (
        jnp.einsum("nihd,njhd->nhij", q_blocks, k_blocks, preferred_element_type=jnp.float32)
        * factor
    )
    probs = jnp.where(causal[None, None], scores, 0.0).astype(jnp.bfloat16)
    attended = jnp.einsum("nhij,njhd->nihd", probs, v_blocks, preferred_element_type=jnp.float32)
    attended = attended + factor * jnp.einsum(
        "nihd,nhde->nihe", q_blocks, prefix_state, preferred_element_type=jnp.float32
    )
    dscores = (
        jnp.einsum("nihe,njhe->nhij", g_blocks, v_blocks, preferred_element_type=jnp.float32)
        * factor
    )
    dprobs = jnp.where(causal[None, None], dscores, 0.0).astype(jnp.bfloat16)
    query_grad = jnp.einsum("nhij,njhd->nihd", dprobs, k_blocks, preferred_element_type=jnp.float32)
    query_grad = query_grad + factor * jnp.einsum(
        "nihe,nhde->nihd", g_blocks, prefix_state, preferred_element_type=jnp.float32
    )
    key_grad = jnp.einsum("nhij,nihd->njhd", dprobs, q_blocks, preferred_element_type=jnp.float32)
    key_grad = key_grad + factor * jnp.einsum(
        "njhe,nhde->njhd", v_blocks, suffix_state, preferred_element_type=jnp.float32
    )
    value_grad = jnp.einsum("nhij,nihe->njhe", probs, g_blocks, preferred_element_type=jnp.float32)
    value_grad = value_grad + factor * jnp.einsum(
        "njhd,nhde->njhe", k_blocks, suffix_state, preferred_element_type=jnp.float32
    )
    flat_shape = (tok_rows, head_count * DH)
    return (
        attended.reshape(flat_shape).astype(jnp.bfloat16),
        query_grad.reshape(flat_shape).astype(jnp.bfloat16),
        key_grad.reshape(flat_shape).astype(jnp.bfloat16),
        value_grad.reshape(flat_shape).astype(jnp.bfloat16),
    )


def solution(mesh):
    placed = (P("seq", "head"), P("seq", "head"), P("seq", "head"), P(("seq", "head"), None))
    return jax.shard_map(
        on_device,
        mesh=mesh,
        in_specs=placed,
        out_specs=(P("seq", "head"), P("seq", "head"), P("seq", "head"), P("seq", "head")),
        check_vma=False,
    )
```

profile of v0, /device:TPU:10, one launch (start us, length us, event | category | flops | bytes accessed | tf_op | source)
XLA Modules:
  0.0 162.2 jit_solution(5630863475420050306)
XLA Ops:
  0.6 0.0 copy-start
  0.6 1.0 copy.28
  1.7 0.0 copy-done
  1.7 0.1 copy.29
  1.8 0.0 copy-start.1
  1.8 0.2 fusion.14
  2.0 1.9 %collective-permute-start = (f32[4,64,64]{2,1,0:T(8,128)S(1)}, f32[4,64,64]{2,1,0:T(8,128)S(1)}, u32[]{:S(2)}, u32[]{:S(2)}) collective-permute-start(f32[4,64,64]{2,1,0:T(8,128)S(1)} %fusion.14), channel_id=1, source_target_pairs={{0,8},{8,16},{16,24},{24,32},{32,40},{40,48},{48,56},{56,64},{64,7... | collective-permute-start | bytes 196616 | tf_op jit(solution)/shard_map/ppermute | solution.py:15
  3.9 0.0 copy-done.1
  3.9 0.7 copy.45
  4.6 7.5 %all-to-all-start = ((bf16[32,8,256]{2,0,1:T(8,128)(2,1)}), bf16[32,8,256]{2,0,1:T(8,128)(2,1)S(1)}, u32[]{:S(2)}, u32[]{:S(2)}) async-start(bf16[32,8,256]{2,0,1:T(8,128)(2,1)} %bitcast.67), calls=%async_computation | async-start | bytes 262144 | tf_op jit(solution)/shard_map/all_to_all | solution.py:23
  12.1 0.0 copy-start.2
  12.1 6.5 %collective-permute-done = f32[4,64,64]{2,1,0:T(8,128)S(1)} collective-permute-done((f32[4,64,64]{2,1,0:T(8,128)S(1)}, f32[4,64,64]{2,1,0:T(8,128)S(1)}, u32[]{:S(2)}, u32[]{:S(2)}) %collective-permute-start) | collective-permute-done | bytes 65568 | tf_op jit(solution)/shard_map/ppermute | solution.py:15
  18.6 1.9 %collective-permute-start.1 = (f32[4,64,64]{2,1,0:T(8,128)S(1)}, f32[4,64,64]{2,1,0:T(8,128)S(1)}, u32[]{:S(2)}, u32[]{:S(2)}) collective-permute-start(f32[4,64,64]{2,1,0:T(8,128)S(1)} %add.74), channel_id=1, source_target_pairs={{0,16},{8,24},{16,32},{24,40},{32,48},{40,56},{48,64},{56,72},{64,... | collective-permute-start | bytes 196616 | tf_op jit(solution)/shard_map/ppermute | solution.py:15
  20.6 0.0 copy-done.2
  20.6 0.1 copy.27
  20.7 9.1 %collective-permute-done.1 = f32[4,64,64]{2,1,0:T(8,128)S(1)} collective-permute-done((f32[4,64,64]{2,1,0:T(8,128)S(1)}, f32[4,64,64]{2,1,0:T(8,128)S(1)}, u32[]{:S(2)}, u32[]{:S(2)}) %collective-permute-start.1) | collective-permute-done | bytes 65568 | tf_op jit(solution)/shard_map/ppermute | solution.py:15
  29.8 1.9 %collective-permute-start.2 = (f32[4,64,64]{2,1,0:T(8,128)S(1)}, f32[4,64,64]{2,1,0:T(8,128)S(1)}, u32[]{:S(2)}, u32[]{:S(2)}) collective-permute-start(f32[4,64,64]{2,1,0:T(8,128)S(1)} %add.75), channel_id=1, source_target_pairs={{0,32},{8,40},{16,48},{24,56},{32,64},{40,72},{48,80},{56,88},{64,... | collective-permute-start | bytes 196616 | tf_op jit(solution)/shard_map/ppermute | solution.py:15
  31.8 9.9 %collective-permute-done.2 = f32[4,64,64]{2,1,0:T(8,128)S(1)} collective-permute-done((f32[4,64,64]{2,1,0:T(8,128)S(1)}, f32[4,64,64]{2,1,0:T(8,128)S(1)}, u32[]{:S(2)}, u32[]{:S(2)}) %collective-permute-start.2) | collective-permute-done | bytes 65568 | tf_op jit(solution)/shard_map/ppermute | solution.py:15
  41.7 1.9 %collective-permute-start.3 = (f32[4,64,64]{2,1,0:T(8,128)S(1)}, f32[4,64,64]{2,1,0:T(8,128)S(1)}, u32[]{:S(2)}, u32[]{:S(2)}) collective-permute-start(f32[4,64,64]{2,1,0:T(8,128)S(1)} %add.76), channel_id=1, source_target_pairs={{0,64},{8,72},{16,80},{24,88},{32,96},{40,104},{48,112},{56,120},{... | collective-permute-start | bytes 196616 | tf_op jit(solution)/shard_map/ppermute | solution.py:15
  43.6 0.0 all-to-all-done
  43.7 0.2 reshape.151
  43.8 0.2 copy.32
  44.0 0.2 fusion.15
  44.2 2.6 %collective-permute-start.7 = (f32[4,64,64]{2,1,0:T(8,128)S(1)}, f32[4,64,64]{2,1,0:T(8,128)S(1)}, u32[]{:S(2)}, u32[]{:S(2)}) collective-permute-start(f32[4,64,64]{2,1,0:T(8,128)S(1)} %fusion.15), channel_id=1, source_target_pairs={{8,0},{16,8},{24,16},{32,24},{40,32},{48,40},{56,48},{64,56},{72,6... | collective-permute-start | bytes 196616 | tf_op jit(solution)/shard_map/ppermute | solution.py:15
  46.8 0.3 fusion.2
  47.1 12.4 %collective-permute-done.3 = f32[4,64,64]{2,1,0:T(8,128)S(1)} collective-permute-done((f32[4,64,64]{2,1,0:T(8,128)S(1)}, f32[4,64,64]{2,1,0:T(8,128)S(1)}, u32[]{:S(2)}, u32[]{:S(2)}) %collective-permute-start.3) | collective-permute-done | bytes 65568 | tf_op jit(solution)/shard_map/ppermute | solution.py:15
  59.5 7.0 %collective-permute-start.4 = (f32[4,64,64]{2,1,0:T(8,128)S(1)}, f32[4,64,64]{2,1,0:T(8,128)S(1)}, u32[]{:S(2)}, u32[]{:S(2)}) collective-permute-start(f32[4,64,64]{2,1,0:T(8,128)S(1)} %add.77), channel_id=1, source_target_pairs={{0,128},{8,136},{16,144},{24,152},{32,160},{40,168},{48,176},{56,1... | collective-permute-start | bytes 196616 | tf_op jit(solution)/shard_map/ppermute | solution.py:15
  66.5 0.0 collective-permute-done.7
  66.6 1.9 %collective-permute-start.8 = (f32[4,64,64]{2,1,0:T(8,128)S(1)}, f32[4,64,64]{2,1,0:T(8,128)S(1)}, u32[]{:S(2)}, u32[]{:S(2)}) collective-permute-start(f32[4,64,64]{2,1,0:T(8,128)S(1)} %add.84), channel_id=1, source_target_pairs={{16,0},{24,8},{32,16},{40,24},{48,32},{56,40},{64,48},{72,56},{80,... | collective-permute-start | bytes 196616 | tf_op jit(solution)/shard_map/ppermute | solution.py:15
  68.5 0.3 convolution_bitcast_fusion.3
  68.8 6.7 %collective-permute-done.4 = f32[4,64,64]{2,1,0:T(8,128)S(1)} collective-permute-done((f32[4,64,64]{2,1,0:T(8,128)S(1)}, f32[4,64,64]{2,1,0:T(8,128)S(1)}, u32[]{:S(2)}, u32[]{:S(2)}) %collective-permute-start.4) | collective-permute-done | bytes 65568 | tf_op jit(solution)/shard_map/ppermute | solution.py:15
  75.5 5.0 %collective-permute-start.5 = (f32[4,64,64]{2,1,0:T(8,128)S(1)}, f32[4,64,64]{2,1,0:T(8,128)S(1)}, u32[]{:S(2)}, u32[]{:S(2)}) collective-permute-start(f32[4,64,64]{2,1,0:T(8,128)S(1)} %add.78), channel_id=1, source_target_pairs={{0,256},{8,264},{16,272},{24,280},{32,288},{40,296},{48,304},{56,3... | collective-permute-start | bytes 196616 | tf_op jit(solution)/shard_map/ppermute | solution.py:15
  80.6 0.0 collective-permute-done.8
  80.6 1.9 %collective-permute-start.9 = (f32[4,64,64]{2,1,0:T(8,128)S(1)}, f32[4,64,64]{2,1,0:T(8,128)S(1)}, u32[]{:S(2)}, u32[]{:S(2)}) collective-permute-start(f32[4,64,64]{2,1,0:T(8,128)S(1)} %add.85), channel_id=1, source_target_pairs={{32,0},{40,8},{48,16},{56,24},{64,32},{72,40},{80,48},{88,56},{96,... | collective-permute-start | bytes 196616 | tf_op jit(solution)/shard_map/ppermute | solution.py:15
  82.6 0.3 fusion.3
  82.9 3.8 %collective-permute-done.5 = f32[4,64,64]{2,1,0:T(8,128)S(1)} collective-permute-done((f32[4,64,64]{2,1,0:T(8,128)S(1)}, f32[4,64,64]{2,1,0:T(8,128)S(1)}, u32[]{:S(2)}, u32[]{:S(2)}) %collective-permute-start.5) | collective-permute-done | bytes 65568 | tf_op jit(solution)/shard_map/ppermute | solution.py:15
  86.8 6.0 %collective-permute-start.6 = (f32[4,64,64]{2,1,0:T(8,128)S(1)}, f32[4,64,64]{2,1,0:T(8,128)S(1)}, u32[]{:S(2)}, u32[]{:S(2)}) collective-permute-start(f32[4,64,64]{2,1,0:T(8,128)S(1)} %add.79), channel_id=1, source_target_pairs={{0,512},{8,520},{16,528},{24,536},{32,544},{40,552},{48,560},{56,5... | collective-permute-start | bytes 196616 | tf_op jit(solution)/shard_map/ppermute | solution.py:15
  92.7 0.0 collective-permute-done.9
  92.8 6.7 %collective-permute-start.10 = (f32[4,64,64]{2,1,0:T(8,128)S(1)}, f32[4,64,64]{2,1,0:T(8,128)S(1)}, u32[]{:S(2)}, u32[]{:S(2)}) collective-permute-start(f32[4,64,64]{2,1,0:T(8,128)S(1)} %add.86), channel_id=1, source_target_pairs={{64,0},{72,8},{80,16},{88,24},{96,32},{104,40},{112,48},{120,56},{... | collective-permute-start | bytes 196616 | tf_op jit(solution)/shard_map/ppermute | solution.py:15
  99.4 0.3 convolution_bitcast_fusion.2
  99.7 11.0 %collective-permute-done.10 = f32[4,64,64]{2,1,0:T(8,128)S(1)} collective-permute-done((f32[4,64,64]{2,1,0:T(8,128)S(1)}, f32[4,64,64]{2,1,0:T(8,128)S(1)}, u32[]{:S(2)}, u32[]{:S(2)}) %collective-permute-start.10) | collective-permute-done | bytes 65568 | tf_op jit(solution)/shard_map/ppermute | solution.py:15
  110.7 10.2 %collective-permute-start.11 = (f32[4,64,64]{2,1,0:T(8,128)S(1)}, f32[4,64,64]{2,1,0:T(8,128)S(1)}, u32[]{:S(2)}, u32[]{:S(2)}) collective-permute-start(f32[4,64,64]{2,1,0:T(8,128)S(1)} %add.87), channel_id=1, source_target_pairs={{128,0},{136,8},{144,16},{152,24},{160,32},{168,40},{176,48},{184,... | collective-permute-start | bytes 196616 | tf_op jit(solution)/shard_map/ppermute | solution.py:15
  121.0 0.0 collective-permute-done.6
  121.0 4.9 %collective-permute-done.11 = f32[4,64,64]{2,1,0:T(8,128)S(1)} collective-permute-done((f32[4,64,64]{2,1,0:T(8,128)S(1)}, f32[4,64,64]{2,1,0:T(8,128)S(1)}, u32[]{:S(2)}, u32[]{:S(2)}) %collective-permute-start.11) | collective-permute-done | bytes 65568 | tf_op jit(solution)/shard_map/ppermute | solution.py:15
  125.9 1.3 collective-permute-start.12
  127.2 0.2 fusion.9
  127.4 13.6 %collective-permute-done.12 = f32[4,64,64]{2,1,0:T(8,128)S(1)} collective-permute-done((f32[4,64,64]{2,1,0:T(8,128)S(1)}, f32[4,64,64]{2,1,0:T(8,128)S(1)}, u32[]{:S(2)}, u32[]{:S(2)}) %collective-permute-start.12) | collective-permute-done | bytes 65568 | tf_op jit(solution)/shard_map/ppermute | solution.py:15
  141.0 1.3 collective-permute-start.13
  142.3 0.2 fusion.8
  142.6 0.8 copy.38
  143.3 0.8 copy.37
  144.1 15.7 %collective-permute-done.13 = f32[4,64,64]{2,1,0:T(8,128)S(1)} collective-permute-done((f32[4,64,64]{2,1,0:T(8,128)S(1)}, f32[4,64,64]{2,1,0:T(8,128)S(1)}, u32[]{:S(2)}, u32[]{:S(2)}) %collective-permute-start.13) | collective-permute-done | bytes 65568 | tf_op jit(solution)/shard_map/ppermute | solution.py:15
  159.8 0.2 convolution_multiply_fusion.2
  160.1 0.2 convolution_multiply_fusion.3
  160.2 0.2 fusion.10
  160.5 0.8 copy.39
  161.2 0.2 fusion.11
  161.4 0.8 copy.40
  (15 shorter events, 0.3 us)
Async XLA Ops:
  0.6 1.1 copy-start
  1.8 2.1 %copy-start.1 = (bf16[32,2048]{1,0:T(8,128)(2,1)S(1)}, bf16[32,2048]{1,0:T(8,128)(2,1)}, u32[]{:S(2)}) copy-start(bf16[32,2048]{1,0:T(8,128)(2,1)} %param.7) | copy-start | bytes 393220
  2.0 16.6 %collective-permute-start = (f32[4,64,64]{2,1,0:T(8,128)S(1)}, f32[4,64,64]{2,1,0:T(8,128)S(1)}, u32[]{:S(2)}, u32[]{:S(2)}) collective-permute-start(f32[4,64,64]{2,1,0:T(8,128)S(1)} %fusion.14), channel_id=1, source_target_pairs={{0,8},{8,16},{16,24},{24,32},{32,40},{40,48},{48,56},{56,64},{64,7... | collective-permute-start | bytes 196616 | tf_op jit(solution)/shard_map/ppermute | solution.py:15
  4.6 39.1 %all-to-all-start = ((bf16[32,8,256]{2,0,1:T(8,128)(2,1)}), bf16[32,8,256]{2,0,1:T(8,128)(2,1)S(1)}, u32[]{:S(2)}, u32[]{:S(2)}) async-start(bf16[32,8,256]{2,0,1:T(8,128)(2,1)} %bitcast.67), calls=%async_computation | async-start | bytes 262144 | tf_op jit(solution)/shard_map/all_to_all | solution.py:23
  12.1 8.4 %copy-start.2 = (bf16[256,256]{1,0:T(8,128)(2,1)S(1)}, bf16[256,256]{1,0:T(8,128)(2,1)}, u32[]{:S(2)}) copy-start(bf16[256,256]{1,0:T(8,128)(2,1)} %param.4) | copy-start | bytes 393220
  18.6 11.1 %collective-permute-start.1 = (f32[4,64,64]{2,1,0:T(8,128)S(1)}, f32[4,64,64]{2,1,0:T(8,128)S(1)}, u32[]{:S(2)}, u32[]{:S(2)}) collective-permute-start(f32[4,64,64]{2,1,0:T(8,128)S(1)} %add.74), channel_id=1, source_target_pairs={{0,16},{8,24},{16,32},{24,40},{32,48},{40,56},{48,64},{56,72},{64,... | collective-permute-start | bytes 196616 | tf_op jit(solution)/shard_map/ppermute | solution.py:15
  29.8 11.9 %collective-permute-start.2 = (f32[4,64,64]{2,1,0:T(8,128)S(1)}, f32[4,64,64]{2,1,0:T(8,128)S(1)}, u32[]{:S(2)}, u32[]{:S(2)}) collective-permute-start(f32[4,64,64]{2,1,0:T(8,128)S(1)} %add.75), channel_id=1, source_target_pairs={{0,32},{8,40},{16,48},{24,56},{32,64},{40,72},{48,80},{56,88},{64,... | collective-permute-start | bytes 196616 | tf_op jit(solution)/shard_map/ppermute | solution.py:15
  41.7 17.8 %collective-permute-start.3 = (f32[4,64,64]{2,1,0:T(8,128)S(1)}, f32[4,64,64]{2,1,0:T(8,128)S(1)}, u32[]{:S(2)}, u32[]{:S(2)}) collective-permute-start(f32[4,64,64]{2,1,0:T(8,128)S(1)} %add.76), channel_id=1, source_target_pairs={{0,64},{8,72},{16,80},{24,88},{32,96},{40,104},{48,112},{56,120},{... | collective-permute-start | bytes 196616 | tf_op jit(solution)/shard_map/ppermute | solution.py:15
  44.2 22.4 %collective-permute-start.7 = (f32[4,64,64]{2,1,0:T(8,128)S(1)}, f32[4,64,64]{2,1,0:T(8,128)S(1)}, u32[]{:S(2)}, u32[]{:S(2)}) collective-permute-start(f32[4,64,64]{2,1,0:T(8,128)S(1)} %fusion.15), channel_id=1, source_target_pairs={{8,0},{16,8},{24,16},{32,24},{40,32},{48,40},{56,48},{64,56},{72,6... | collective-permute-start | bytes 196616 | tf_op jit(solution)/shard_map/ppermute | solution.py:15
  59.5 16.0 %collective-permute-start.4 = (f32[4,64,64]{2,1,0:T(8,128)S(1)}, f32[4,64,64]{2,1,0:T(8,128)S(1)}, u32[]{:S(2)}, u32[]{:S(2)}) collective-permute-start(f32[4,64,64]{2,1,0:T(8,128)S(1)} %add.77), channel_id=1, source_target_pairs={{0,128},{8,136},{16,144},{24,152},{32,160},{40,168},{48,176},{56,1... | collective-permute-start | bytes 196616 | tf_op jit(solution)/shard_map/ppermute | solution.py:15
  66.6 14.0 %collective-permute-start.8 = (f32[4,64,64]{2,1,0:T(8,128)S(1)}, f32[4,64,64]{2,1,0:T(8,128)S(1)}, u32[]{:S(2)}, u32[]{:S(2)}) collective-permute-start(f32[4,64,64]{2,1,0:T(8,128)S(1)} %add.84), channel_id=1, source_target_pairs={{16,0},{24,8},{32,16},{40,24},{48,32},{56,40},{64,48},{72,56},{80,... | collective-permute-start | bytes 196616 | tf_op jit(solution)/shard_map/ppermute | solution.py:15
  75.5 11.2 %collective-permute-start.5 = (f32[4,64,64]{2,1,0:T(8,128)S(1)}, f32[4,64,64]{2,1,0:T(8,128)S(1)}, u32[]{:S(2)}, u32[]{:S(2)}) collective-permute-start(f32[4,64,64]{2,1,0:T(8,128)S(1)} %add.78), channel_id=1, source_target_pairs={{0,256},{8,264},{16,272},{24,280},{32,288},{40,296},{48,304},{56,3... | collective-permute-start | bytes 196616 | tf_op jit(solution)/shard_map/ppermute | solution.py:15
  80.6 12.1 %collective-permute-start.9 = (f32[4,64,64]{2,1,0:T(8,128)S(1)}, f32[4,64,64]{2,1,0:T(8,128)S(1)}, u32[]{:S(2)}, u32[]{:S(2)}) collective-permute-start(f32[4,64,64]{2,1,0:T(8,128)S(1)} %add.85), channel_id=1, source_target_pairs={{32,0},{40,8},{48,16},{56,24},{64,32},{72,40},{80,48},{88,56},{96,... | collective-permute-start | bytes 196616 | tf_op jit(solution)/shard_map/ppermute | solution.py:15
  86.8 34.2 %collective-permute-start.6 = (f32[4,64,64]{2,1,0:T(8,128)S(1)}, f32[4,64,64]{2,1,0:T(8,128)S(1)}, u32[]{:S(2)}, u32[]{:S(2)}) collective-permute-start(f32[4,64,64]{2,1,0:T(8,128)S(1)} %add.79), channel_id=1, source_target_pairs={{0,512},{8,520},{16,528},{24,536},{32,544},{40,552},{48,560},{56,5... | collective-permute-start | bytes 196616 | tf_op jit(solution)/shard_map/ppermute | solution.py:15
  92.8 18.0 %collective-permute-start.10 = (f32[4,64,64]{2,1,0:T(8,128)S(1)}, f32[4,64,64]{2,1,0:T(8,128)S(1)}, u32[]{:S(2)}, u32[]{:S(2)}) collective-permute-start(f32[4,64,64]{2,1,0:T(8,128)S(1)} %add.86), channel_id=1, source_target_pairs={{64,0},{72,8},{80,16},{88,24},{96,32},{104,40},{112,48},{120,56},{... | collective-permute-start | bytes 196616 | tf_op jit(solution)/shard_map/ppermute | solution.py:15
  110.7 15.1 %collective-permute-start.11 = (f32[4,64,64]{2,1,0:T(8,128)S(1)}, f32[4,64,64]{2,1,0:T(8,128)S(1)}, u32[]{:S(2)}, u32[]{:S(2)}) collective-permute-start(f32[4,64,64]{2,1,0:T(8,128)S(1)} %add.87), channel_id=1, source_target_pairs={{128,0},{136,8},{144,16},{152,24},{160,32},{168,40},{176,48},{184,... | collective-permute-start | bytes 196616 | tf_op jit(solution)/shard_map/ppermute | solution.py:15
  125.9 15.1 %collective-permute-start.12 = (f32[4,64,64]{2,1,0:T(8,128)S(1)}, f32[4,64,64]{2,1,0:T(8,128)S(1)}, u32[]{:S(2)}, u32[]{:S(2)}) collective-permute-start(f32[4,64,64]{2,1,0:T(8,128)S(1)} %add.88), channel_id=1, source_target_pairs={{256,0},{264,8},{272,16},{280,24},{288,32},{296,40},{304,48},{312,... | collective-permute-start | bytes 196616 | tf_op jit(solution)/shard_map/ppermute | solution.py:15
  141.0 18.8 %collective-permute-start.13 = (f32[4,64,64]{2,1,0:T(8,128)S(1)}, f32[4,64,64]{2,1,0:T(8,128)S(1)}, u32[]{:S(2)}, u32[]{:S(2)}) collective-permute-start(f32[4,64,64]{2,1,0:T(8,128)S(1)} %add.89), channel_id=1, source_target_pairs={{512,0},{520,8},{528,16},{536,24},{544,32},{552,40},{560,48},{568,... | collective-permute-start | bytes 196616 | tf_op jit(solution)/shard_map/ppermute | solution.py:15
where the time goes:
time: 163 us; the launch traced here: 162 us
  waiting for transfers between devices  93.7 us (57%)
  starting transfers between devices  59.1 us (36%)
  local copies, waits for them, and re-layouts  5.27 us (3%)
  matrix products  2.77 us (2%)
    ppermute x14, waiting for transfers between devices, passed_along(): lax.ppermute(value, axis, [(source, source + steps) for source in range(i...  93.7 us
    ppermute x14, starting transfers between devices, passed_along(): lax.ppermute(value, axis, [(source, source + steps) for source in range(i...  51.6 us
    all_to_all x1, starting transfers between devices, on_device(): lax.all_to_all(out_grad, 'head', split_axis=1, concat_axis=0, tiled=True)  7.54 us
    unnamed x13, local copies, waits for them, and re-layouts  4.29 us
  transfers between devices with their start and end apart: 15, of which 10 were waited for; matrix products, arithmetic and copies ran while one was open for 3% of the time, Pallas kernels for 0%

commit v1 on v0

v1 whole, which is shorter than its diff:
```python
import functools
import math

import jax
import jax.numpy as jnp
from jax import lax
from jax.experimental import pallas as pl
from jax.experimental.pallas import tpu as pltpu
from jax.sharding import PartitionSpec as P

DH = 64
BLOCK = 256
PAIR = 2 * DH
MESH = pl.DeviceIdType.MESH

NX = 4
QUADS = 3
QUAD = 4

F32 = jnp.float32
BF16 = jnp.bfloat16


def dot(a, b):
    return lax.dot_general(a, b, (((1,), (0,)), ((), ())), preferred_element_type=F32)


def dot_t(a, b):
    return lax.dot_general(a, b, (((1,), (1,)), ((), ())), preferred_element_type=F32)


def t_dot(a, b):
    return lax.dot_general(a, b, (((0,), (0,)), ((), ())), preferred_element_type=F32)


def lane_half(shape):
    return lax.broadcasted_iota(jnp.int32, shape, 1) < DH


def compact(state):
    return jnp.where(lane_half((DH, PAIR)), state[:DH], state[DH:])


def spread(state):
    first = lane_half((DH, PAIR))
    zero = jnp.zeros_like(state)
    return jnp.concatenate([jnp.where(first, state, zero), jnp.where(first, zero, state)], 0)


def halves(a):
    first = lane_half(a.shape)
    zero = jnp.zeros_like(a)
    return jnp.where(first, a, zero), jnp.where(first, zero, a)


def carry_kernel(
    factor, ny,
    q_hbm, k_hbm, v_hbm, g_hbm,
    att, qg, kg_part, vg_part, k, v, suffix,
    q, g_rows, g, probs_t, att_part, qg_hold, local,
    state, core_in, chip_out, quad_in, quad_out, line_in, line_out, x_in, final_out, carried,
    load_sem, a2a_send, a2a_recv, send_sem, recv_sem,
):
    nz = QUADS * QUAD
    seq, head = lax.axis_index("seq"), lax.axis_index("head")
    core, chip = seq % 2, seq // 2
    x, z = chip // nz, chip % nz
    run, place = z // QUAD, z % QUAD
    rows = BLOCK // ny

    def at(x, run, place, core):
        return ((x * QUADS + run) * QUAD + place) * 2 + core

    mate = at(x, run, place, 1 - core)
    quad_mates = [at(x, run, (place + i) % QUAD, core) for i in range(1, QUAD)]
    line_mates = [at(x, (run + i) % QUADS, place, core) for i in range(1, QUADS)]
    x_mates = [at((x + i) % NX, run, place, core) for i in range(1, NX)]

    barrier = pltpu.get_barrier_semaphore()
    greeted = [mate] + quad_mates + line_mates + x_mates
    for other in range(1, ny):
        pl.semaphore_signal(
            barrier, inc=1, device_id=(seq, (head + other) % ny), device_id_type=MESH
        )
    for other in greeted:
        pl.semaphore_signal(barrier, inc=1, device_id=(other, head), device_id_type=MESH)

    loads = [
        pltpu.make_async_copy(src, dst, load_sem.at[i])
        for i, (src, dst) in enumerate(
            [(k_hbm, k), (v_hbm, v), (g_hbm, g_rows), (q_hbm, q)]
        )
    ]
    for load in loads:
        load.start()
    loads[0].wait()
    loads[1].wait()

    lanes = [pl.ds(p * PAIR, PAIR) for p in range(2)]
    for p in range(2):
        state[0, p] = compact(t_dot(k[:, lanes[p]], v[:, lanes[p]]))

    loads[2].wait()
    pl.semaphore_wait(barrier, ny - 1 + len(greeted))

    width = 2 * PAIR
    mine = pl.ds(pl.multiple_of(head * rows, rows), rows)
    exchange = []
    for i in sorted(range(1, ny), key=lambda i: -min(i, ny - i)):
        there = (head + i) % ny
        exchange.append(
            pltpu.make_async_remote_copy(
                src_ref=g_rows.at[:, pl.ds(pl.multiple_of(there * width, width), width)],
                dst_ref=g.at[mine, :],
                send_sem=a2a_send.at[i - 1],
                recv_sem=a2a_recv.at[i - 1],
                device_id=(seq, there),
                device_id_type=MESH,
            )
        )
        exchange[-1].start()
    own = pltpu.make_async_copy(
        g_rows.at[:, pl.ds(pl.multiple_of(head * width, width), width)],
        g.at[mine, :],
        load_sem.at[4],
    )
    own.start()

    sent = []

    def send(src, dst, slot, to):
        copy = pltpu.make_async_remote_copy(
            src_ref=src,
            dst_ref=dst,
            send_sem=send_sem.at[slot],
            recv_sem=recv_sem.at[slot],
            device_id=(to, head),
            device_id_type=MESH,
        )
        copy.start()
        sent.append(copy)
        return copy

    per_way = 2 + (QUAD - 1) + (QUADS - 1) + (NX - 1)

    def before(way, there, here):
        return there < here if way == 0 else there > here

    def masked(flag, value):
        return jnp.where(flag, value, jnp.zeros_like(value))

    def to_core(way):
        return [send(state.at[way, 1 - core], core_in.at[way], way * per_way, mate)]

    def to_quad(way, copies):
        copies[0].wait_recv()
        total = state[way, core] + core_in[way]
        local[way, 0] = total
        chip_out[way] = total.astype(BF16)
        base = way * per_way + 1
        return [
            send(chip_out.at[way], quad_in.at[way, i], base + i, to)
            for i, to in enumerate(quad_mates)
        ]

    def to_line(way, copies):
        for copy in copies:
            copy.wait_recv()
        total = local[way, 0]
        partial = jnp.zeros_like(total)
        for i in range(QUAD - 1):
            came = quad_in[way, i].astype(F32)
            total = total + came
            partial = partial + masked(before(way, (place - 1 - i) % QUAD, place), came)
        local[way, 0] = total
        local[way, 1] = partial
        quad_out[way] = total.astype(BF16)
        base = way * per_way + 1 + (QUAD - 1)
        return [
            send(quad_out.at[way], line_in.at[way, i], base + i, to)
            for i, to in enumerate(line_mates)
        ]

    def to_x(way, copies):
        for copy in copies:
            copy.wait_recv()
        total, partial = local[way, 0], local[way, 1]
        for i in range(QUADS - 1):
            came = line_in[way, i].astype(F32)
            total = total + came
            partial = partial + masked(before(way, (run - 1 - i) % QUADS, run), came)
        local[way, 1] = partial
        line_out[way] = total.astype(BF16)
        base = way * per_way + 1 + (QUAD - 1) + (QUADS - 1)
        return [
            send(line_out.at[way], x_in.at[way, i], base + i, to) for i, to in enumerate(x_mates)
        ]

    def to_mate(way, copies):
        for copy in copies:
            copy.wait_recv()
        partial = local[way, 1]
        for i in range(NX - 1):
            came = x_in[way, i].astype(F32)
            partial = partial + masked(before(way, (x - 1 - i) % NX, x), came)
        carries = core == 1 - way
        here = partial + masked(carries, core_in[way])
        there = partial + masked(jnp.logical_not(carries), state[way, core])
        final_out[way] = there.astype(BF16)
        copy = send(
            final_out.at[way], carried.at[way, core], way * per_way + per_way - 1, mate
        )
        carried[way, core] = here.astype(BF16)
        return [copy]

    row = lax.broadcasted_iota(jnp.int32, (BLOCK, BLOCK), 0)
    col = lax.broadcasted_iota(jnp.int32, (BLOCK, BLOCK), 1)
    lower, upper = row >= col, row <= col

    def weights(a, b, keep):
        return jnp.where(keep, dot_t(a, b) * factor, 0.0).astype(BF16)

    def forward_part():
        for p in range(2):
            qs, ks, vs = q[:, lanes[p]], k[:, lanes[p]], v[:, lanes[p]]
            kh, vh = halves(ks), halves(vs)
            total = jnp.zeros((BLOCK, PAIR), F32)
            for h in range(2):
                total += dot(weights(qs, kh[h], lower), vh[h])
                probs_t[2 * p + h] = weights(kh[h], qs, upper)
            att_part[:, lanes[p]] = total

    def backward_part():
        for p in range(2):
            qs, ks, vs, gs = (a[:, lanes[p]] for a in (q, k, v, g))
            qh, kh, vh, gh = halves(qs), halves(ks), halves(vs), halves(gs)
            q_sum = jnp.zeros((BLOCK, PAIR), F32)
            k_sum = jnp.zeros((BLOCK, PAIR), F32)
            v_sum = jnp.zeros((BLOCK, PAIR), F32)
            for h in range(2):
                q_sum += dot(weights(gs, vh[h], lower), kh[h])
                k_sum += dot(weights(vh[h], gs, upper), qh[h])
                v_sum += dot(probs_t[2 * p + h], gh[h])
            qg_hold[:, lanes[p]] = q_sum
            kg_part[:, lanes[p]] = k_sum
            vg_part[:, lanes[p]] = v_sum

    forward = to_core(0)
    forward = to_quad(0, forward)
    loads[3].wait()
    forward_part()
    forward = to_line(0, forward)

    own.wait()
    for copy in exchange:
        copy.wait_recv()
    for p in range(2):
        state[1, p] = compact(t_dot(q[:, lanes[p]], g[:, lanes[p]]))
    backward = to_core(1)
    backward = to_quad(1, backward)
    forward = to_x(0, forward)
    backward_part()
    backward = to_line(1, backward)
    forward = to_mate(0, forward)
    forward[0].wait_recv()
    for p in range(2):
        prefix = spread(carried[0, p])
        att[:, lanes[p]] = (att_part[:, lanes[p]] + factor * dot(q[:, lanes[p]], prefix)).astype(BF16)
        qg[:, lanes[p]] = (qg_hold[:, lanes[p]] + factor * dot_t(g[:, lanes[p]], prefix)).astype(BF16)
    backward = to_x(1, backward)
    backward = to_mate(1, backward)
    for copy in exchange + sent:
        copy.wait_send()
    backward[0].wait_recv()
    suffix[...] = carried[1]


def finish_kernel(factor, att_in, qg_in, kg_part, vg_part, k, v, suffix, att, qg, kg, vg, kg_out, vg_out, sem):
    done = [
        pltpu.make_async_copy(att_in, att, sem.at[0]),
        pltpu.make_async_copy(qg_in, qg, sem.at[1]),
    ]
    for copy in done:
        copy.start()
    for p in range(2):
        lanes = pl.ds(p * PAIR, PAIR)
        later = spread(suffix[p])
        kg_out[:, lanes] = (kg_part[:, lanes] + factor * dot_t(v[:, lanes], later)).astype(BF16)
        vg_out[:, lanes] = (vg_part[:, lanes] + factor * dot(k[:, lanes], later)).astype(BF16)
    for i, (src, dst) in enumerate([(kg_out, kg), (vg_out, vg)]):
        done.append(pltpu.make_async_copy(src, dst, sem.at[2 + i]))
        done[-1].start()
    for copy in done:
        copy.wait()


def on_device(queries, keys, values, out_grad):
    ny = lax.axis_size("head")
    tokens = queries.shape[0] * lax.axis_size("seq")
    factor = 1.0 / math.sqrt(DH * tokens)
    wide = queries.shape
    vmem = pl.BlockSpec(memory_space=pltpu.VMEM)
    hbm = pl.BlockSpec(memory_space=pltpu.HBM)
    messages = 2 * (2 + (QUAD - 1) + (QUADS - 1) + (NX - 1))
    pair = (DH, PAIR)
    held = pl.pallas_call(
        functools.partial(carry_kernel, factor, ny),
        out_shape=[
            jax.ShapeDtypeStruct(wide, BF16),
            jax.ShapeDtypeStruct(wide, BF16),
            jax.ShapeDtypeStruct(wide, F32),
            jax.ShapeDtypeStruct(wide, F32),
            jax.ShapeDtypeStruct(wide, BF16),
            jax.ShapeDtypeStruct(wide, BF16),
            jax.ShapeDtypeStruct((2,) + pair, BF16),
        ],
        in_specs=[hbm] * 4,
        out_specs=[vmem] * 7,
        scratch_shapes=[
            pltpu.VMEM(wide, BF16),
            pltpu.VMEM(out_grad.shape, BF16),
            pltpu.VMEM(wide, BF16),
            pltpu.VMEM((4, BLOCK, BLOCK), BF16),
            pltpu.VMEM(wide, F32),
            pltpu.VMEM(wide, F32),
            pltpu.VMEM((2, 2) + pair, F32),
            pltpu.VMEM((2, 2) + pair, F32),
            pltpu.VMEM((2,) + pair, F32),
            pltpu.VMEM((2,) + pair, BF16),
            pltpu.VMEM((2, QUAD - 1) + pair, BF16),
            pltpu.VMEM((2,) + pair, BF16),
            pltpu.VMEM((2, QUADS - 1) + pair, BF16),
            pltpu.VMEM((2,) + pair, BF16),
            pltpu.VMEM((2, NX - 1) + pair, BF16),
            pltpu.VMEM((2,) + pair, BF16),
            pltpu.VMEM((2, 2) + pair, BF16),
            pltpu.SemaphoreType.DMA((5,)),
            pltpu.SemaphoreType.DMA((ny - 1,)),
            pltpu.SemaphoreType.DMA((ny - 1,)),
            pltpu.SemaphoreType.DMA((messages,)),
            pltpu.SemaphoreType.DMA((messages,)),
        ],
        compiler_params=pltpu.CompilerParams(
            collective_id=0, has_side_effects=True, vmem_limit_bytes=16 << 20
        ),
        name="carry",
    )(*[pltpu.with_memory_space_constraint(a, pltpu.HBM) for a in (queries, keys, values, out_grad)])
    return pl.pallas_call(
        functools.partial(finish_kernel, factor),
        out_shape=[jax.ShapeDtypeStruct(wide, BF16)] * 4,
        in_specs=[vmem] * 7,
        out_specs=[hbm] * 4,
        scratch_shapes=[
            pltpu.VMEM(wide, BF16),
            pltpu.VMEM(wide, BF16),
            pltpu.SemaphoreType.DMA((4,)),
        ],
        compiler_params=pltpu.CompilerParams(vmem_limit_bytes=16 << 20),
        name="finish",
    )(*held)


def solution(mesh):
    split = P("seq", "head")
    return jax.shard_map(
        on_device,
        mesh=mesh,
        in_specs=(split, split, split, P(("seq", "head"), None)),
        out_specs=(split, split, split, split),
        check_vma=False,
    )
```

time: 163 us -> 42.9 us (0.26)
  the two profiles are of different devices: /device:TPU:10 before, /device:TPU:1 now
where the time goes in v1:
time: 42.9 us; the launch traced here: 42.8 us
  Pallas kernels  42.1 us (98%)
  between operations  0.64 us (1%)
    pallas_call x1, Pallas kernels, on_device(): pl.pallas_call(functools.partial(carry_kernel, factor, ny), out_shape=[ja...  41.2 us
    pallas_call x1, Pallas kernels, on_device(): pl.pallas_call(functools.partial(finish_kernel, factor), out_shape=[jax.S...  0.95 us

profile of v1, /device:TPU:1, one launch (start us, length us, event | category | flops | bytes accessed | tf_op | source)
XLA Modules:
  0.0 42.8 jit_solution(1126863333069452528)
XLA Ops:
  0.6 41.2 %carry.1 = (bf16[256,256]{1,0:T(8,128)(2,1)S(1)}, bf16[256,256]{1,0:T(8,128)(2,1)S(1)}, f32[256,256]{1,0:T(8,128)S(1)}, f32[256,256]{1,0:T(8,128)S(1)}, bf16[256...) custom-call(bf16[256,256]{1,0:T(8,128)(2,1)} %q_hbm.1, ...), custom_call_target="tpu_custom_call" | custom-call | tf_op jit(solution)/shard_map/carry/pallas_call | solution.py:306
  41.8 1.0 %finish.1 = (bf16[256,256]{1,0:T(8,128)(2,1)}, bf16[256,256]{1,0:T(8,128)(2,1)}, bf16[256,256]{1,0:T(8,128)(2,1)}, bf16[256,256]{1,0:T(8,128)(2,1)}) custom-call(bf16[256,256]{1,0:T(8,128)(2,1)S(1)} %get-tuple-element.11.att_in, bf16[256,256]{1,0:T(8,128)(2,1)S(1)} %get-tuple-element.12.qg_in, f32[256,256]{1,0:T(8,128)S(1)} %get-tuple-element.13.kg_part, ...), custom_call_target="tpu_custom_call" | custom-call | tf_op jit(solution)/shard_map/finish/pallas_call | solution.py:348

commit v2 on v1

v2 whole, which is shorter than its diff:
```python
import functools
import math

import jax
import jax.numpy as jnp
from jax import lax
from jax.experimental import pallas as pl
from jax.experimental.pallas import tpu as pltpu
from jax.sharding import PartitionSpec as P

DH = 64
BLOCK = 256
PAIR = 2 * DH
MESH = pl.DeviceIdType.MESH

NX = 4
QUADS = 3
QUAD = 4
NZ = QUADS * QUAD
REACH = 4
ROUNDS = 1

F32 = jnp.float32
BF16 = jnp.bfloat16


def dot(a, b):
    return lax.dot_general(a, b, (((1,), (0,)), ((), ())), preferred_element_type=F32)


def dot_t(a, b):
    return lax.dot_general(a, b, (((1,), (1,)), ((), ())), preferred_element_type=F32)


def t_dot(a, b):
    return lax.dot_general(a, b, (((0,), (0,)), ((), ())), preferred_element_type=F32)


def lane_half(shape):
    return lax.broadcasted_iota(jnp.int32, shape, 1) < DH


def compact(state):
    return jnp.where(lane_half((DH, PAIR)), state[:DH], state[DH:])


def spread(state):
    first = lane_half((DH, PAIR))
    zero = jnp.zeros_like(state)
    return jnp.concatenate([jnp.where(first, state, zero), jnp.where(first, zero, state)], 0)


def halves(a):
    first = lane_half(a.shape)
    zero = jnp.zeros_like(a)
    return jnp.where(first, a, zero), jnp.where(first, zero, a)


def carry_kernel(
    factor, ny,
    q_hbm, k_hbm, v_hbm, g_hbm,
    att, qg, kg_part, vg_part, k, v, suffix,
    q, q_mate, g_pair, g, probs_t, att_part, qg_part,
    state, core_in, chip, chip_out, quad_in, sums, quad_out, line_in, z_in, x_out, x_in, rest_out, rest_in, total,
    load_sem, a2a_send, a2a_recv, core_send, core_recv, quad_send, quad_recv, line_send, line_recv, z_send, z_recv, x_send, x_recv,
    rest_send, rest_recv, heard,
):
    seq, head = lax.axis_index("seq"), lax.axis_index("head")
    core, chip_id = seq % 2, seq // 2
    x, z = chip_id // NZ, chip_id % NZ
    run, place = z // QUAD, z % QUAD
    rows = BLOCK // ny

    def at(x, z, core):
        return (x * NZ + z) * 2 + core

    mate = at(x, z, 1 - core)

    barrier = pltpu.get_barrier_semaphore()
    greeted = [(to, (head + i) % ny) for i in range(1, ny) for to in (seq, mate)] + [(mate, head)]
    near = sorted({i % NZ for i in range(-REACH, REACH + 1)} - {0})
    greeted += [(at(x, (z + i) % NZ, core), head) for i in near]
    greeted += [(at((x + i) % NX, z, c), head) for i in range(1, NX) for c in range(2)]
    for other in greeted:
        pl.semaphore_signal(barrier, inc=1, device_id=other, device_id_type=MESH)

    loads = [
        pltpu.make_async_copy(src, dst, load_sem.at[i])
        for i, (src, dst) in enumerate(
            [(k_hbm, k), (v_hbm, v), (q_hbm, q)]
        )
    ]
    for load in loads:
        load.start()
    pl.semaphore_wait(barrier, len(greeted))

    def tell(turn):
        for i, step in enumerate((REACH, NZ - REACH)):
            to = (at(x, (z + step) % NZ, core), head)
            pl.semaphore_signal(heard.at[turn, i], inc=1, device_id=to, device_id_type=MESH)

    def hear(turn):
        for i in range(2):
            pl.semaphore_wait(heard.at[turn, i], 1)

    mine = pl.ds(pl.multiple_of(head * rows, rows), rows)

    def columns(group, pair):
        return pl.ds(pl.multiple_of((2 * group + pair) * PAIR, PAIR), PAIR)

    exchange = []
    for i in sorted(range(ny), key=lambda i: -min(i, ny - i)):
        there = (head + i) % ny
        for j in range(2):
            if i == 0 and j == 0:
                continue
            exchange.append(
                pltpu.make_async_remote_copy(
                    src_ref=g_hbm.at[:, columns(there, (core + j) % 2)],
                    dst_ref=g_pair.at[core, mine, :],
                    send_sem=a2a_send.at[2 * i + j],
                    recv_sem=a2a_recv.at[2 * i + j],
                    device_id=(at(x, z, (core + j) % 2), there),
                    device_id_type=MESH,
                )
            )
            exchange[-1].start()
    own = pltpu.make_async_copy(
        g_hbm.at[:, columns(head, core)], g_pair.at[core, mine, :], load_sem.at[4]
    )
    own.start()
    tell(0)

    loads[0].wait()
    loads[1].wait()

    lanes = [pl.ds(p * PAIR, PAIR) for p in range(2)]
    for p in range(2):
        state[0, p] = compact(t_dot(k[:, lanes[p]], v[:, lanes[p]]))


    sent = []

    def send(src, dst, send_sem, recv_sem, to, when=None):
        copy = pltpu.make_async_remote_copy(
            src_ref=src,
            dst_ref=dst,
            send_sem=send_sem,
            recv_sem=recv_sem,
            device_id=(to, head),
            device_id_type=MESH,
        )
        if when is None:
            copy.start()
        else:
            pl.when(when)(copy.start)
        sent.append((when, copy))
        return copy

    def arrived(ref, sem):
        pltpu.make_async_copy(ref, ref, sem).wait()

    def masked(flag, value):
        return jnp.where(flag, value, jnp.zeros_like(value))

    def before(way, there, here):
        return there < here if way == 0 else there > here

    def half(core):
        return pl.ds(pl.multiple_of(core * PAIR, PAIR), PAIR)

    def chip_sum(way):
        both = state[way, core] + core_in[way]
        chip[way] = both
        chip_out[way] = both.astype(BF16)

    def to_quad():
        arrived(core_in.at[0], core_recv.at[0])
        chip_sum(0)
        for i in range(QUAD - 1):
            send(
                chip_out.at[0], quad_in.at[i], quad_send.at[i], quad_recv.at[i],
                at(x, run * QUAD + (place + 1 + i) % QUAD, core),
            )

    def to_line():
        for i in range(QUAD - 1):
            arrived(quad_in.at[i], quad_recv.at[i])
        whole = chip[0]
        partial = jnp.zeros((DH, PAIR), F32)
        for i in range(QUAD - 1):
            came = quad_in[i].astype(F32)
            whole += came
            partial += masked((place - 1 - i) % QUAD < place, came)
        sums[0] = whole
        sums[1] = partial
        quad_out[...] = whole.astype(BF16)
        for i in range(QUADS - 1):
            send(
                quad_out, line_in.at[i], line_send.at[i], line_recv.at[i],
                at(x, (run + 1 + i) % QUADS * QUAD + place, core),
            )

    def earlier():
        for i in range(QUADS - 1):
            arrived(line_in.at[i], line_recv.at[i])
        whole, partial = sums[0], sums[1]
        for i in range(QUADS - 1):
            came = line_in[i].astype(F32)
            whole += came
            partial += masked((run - 1 - i) % QUADS < run, came)
        return whole, partial

    def to_all():
        chip_sum(1)
        for there in range(NZ):
            send(
                chip_out.at[1], z_in.at[z], z_send.at[there], z_recv.at[z], at(x, there, core),
                jnp.logical_or(there < z, jnp.logical_and(there > z, x > 0)),
            )

    def later():
        whole_acc = sums.at[2]
        part_acc = sums.at[3]
        whole_acc[...] = chip[1]
        part_acc[...] = jnp.zeros((DH, PAIR), F32)
        for there in range(NZ):

            @pl.when(there > z)
            def _():
                arrived(z_in.at[there], z_recv.at[there])
                came = z_in[there].astype(F32)
                whole_acc[...] += came
                part_acc[...] += came

            @pl.when(jnp.logical_and(there < z, x > 0))
            def _():
                arrived(z_in.at[there], z_recv.at[there])
                whole_acc[...] += z_in[there].astype(F32)

        return whole_acc[...], part_acc[...]

    def to_x(way):
        whole, partial = (earlier, later)[way]()
        x_out[way] = whole.astype(BF16)
        for there in range(NX):
            for c in range(2):
                send(
                    x_out.at[way], x_in.at[way, core, x],
                    x_send.at[way, there, c], x_recv.at[way, core, x],
                    at(there, z, c), before(way, x, there),
                )
        carries = core == 1 - way
        total[way, core] = partial + masked(carries, core_in[way])
        rest_out[way] = partial + masked(jnp.logical_not(carries), state[way, core])
        send(rest_out.at[way], rest_in.at[way], rest_send.at[way], rest_recv.at[way], mate)

    def finish(way):
        arrived(rest_in.at[way], rest_recv.at[way])
        total[way, 1 - core] = rest_in[way]
        for there in range(NX):

            @pl.when(before(way, there, x))
            def _():
                for p in range(2):
                    arrived(x_in.at[way, p, there], x_recv.at[way, p, there])
                for p in range(2):
                    total[way, p] += x_in[way, p, there].astype(F32)

    row = lax.broadcasted_iota(jnp.int32, (BLOCK, BLOCK), 0)
    col = lax.broadcasted_iota(jnp.int32, (BLOCK, BLOCK), 1)
    lower, upper = row >= col, row <= col

    def weights(a, b, keep):
        return jnp.where(keep, dot_t(a, b) * factor, 0.0).astype(BF16)

    def forward_part():
        for p in range(2):
            qs, ks, vs = q[:, lanes[p]], k[:, lanes[p]], v[:, lanes[p]]
            kh, vh = halves(ks), halves(vs)
            acc = jnp.zeros((BLOCK, PAIR), F32)
            for h in range(2):
                acc += dot(weights(qs, kh[h], lower), vh[h])
                probs_t[2 * p + h] = weights(kh[h], qs, upper)
            att_part[:, lanes[p]] = acc

    def backward_part():
        for p in range(2):
            qs, ks, vs = (a[:, lanes[p]] for a in (q, k, v))
            gs = g[p]
            qh, kh, vh, gh = halves(qs), halves(ks), halves(vs), halves(gs)
            q_sum = jnp.zeros((BLOCK, PAIR), F32)
            k_sum = jnp.zeros((BLOCK, PAIR), F32)
            v_sum = jnp.zeros((BLOCK, PAIR), F32)
            for h in range(2):
                q_sum += dot(weights(gs, vh[h], lower), kh[h])
                k_sum += dot(weights(vh[h], gs, upper), qh[h])
                v_sum += dot(probs_t[2 * p + h], gh[h])
            qg_part[:, lanes[p]] = q_sum
            kg_part[:, lanes[p]] = k_sum
            vg_part[:, lanes[p]] = v_sum

    send(state.at[0, 1 - core], core_in.at[0], core_send.at[0], core_recv.at[0], mate)
    loads[2].wait()
    send(q.at[:, half(1 - core)], q_mate, core_send.at[1], core_recv.at[1], mate)
    forward_part()
    to_quad()
    for turn in range(ROUNDS):
        hear(turn)
        if turn + 1 < ROUNDS:
            tell(turn + 1)
    to_line()

    arrived(q_mate, core_recv.at[1])
    own.wait()
    for copy in exchange:
        copy.wait_recv()
    state[1, core] = compact(t_dot(q[:, half(core)], g_pair[core]))
    core_in[1] = compact(t_dot(q_mate[...], g_pair[1 - core]))
    to_all()
    send(g_pair.at[1 - core], g.at[core], core_send.at[2], core_recv.at[2], mate)
    g[core] = g_pair[core]
    arrived(g.at[1 - core], core_recv.at[2])
    backward_part()

    to_x(0)
    to_x(1)
    finish(0)
    for p in range(2):
        prefix = spread(total[0, p].astype(BF16))
        att[:, lanes[p]] = (att_part[:, lanes[p]] + factor * dot(q[:, lanes[p]], prefix)).astype(BF16)
        qg[:, lanes[p]] = (qg_part[:, lanes[p]] + factor * dot_t(g[p], prefix)).astype(BF16)
    for copy in exchange:
        copy.wait_send()
    for when, copy in sent:
        if when is None:
            copy.wait_send()
        else:
            pl.when(when)(copy.wait_send)
    finish(1)
    suffix[...] = total[1].astype(BF16)


def finish_kernel(factor, att_in, qg_in, kg_part, vg_part, k, v, suffix, att, qg, kg, vg, kg_out, vg_out, sem):
    done = [
        pltpu.make_async_copy(att_in, att, sem.at[0]),
        pltpu.make_async_copy(qg_in, qg, sem.at[1]),
    ]
    for copy in done:
        copy.start()
    for p in range(2):
        lanes = pl.ds(p * PAIR, PAIR)
        later = spread(suffix[p])
        kg_out[:, lanes] = (kg_part[:, lanes] + factor * dot_t(v[:, lanes], later)).astype(BF16)
        vg_out[:, lanes] = (vg_part[:, lanes] + factor * dot(k[:, lanes], later)).astype(BF16)
    for i, (src, dst) in enumerate([(kg_out, kg), (vg_out, vg)]):
        done.append(pltpu.make_async_copy(src, dst, sem.at[2 + i]))
        done[-1].start()
    for copy in done:
        copy.wait()


def on_device(queries, keys, values, out_grad):
    ny = lax.axis_size("head")
    tokens = queries.shape[0] * lax.axis_size("seq")
    factor = 1.0 / math.sqrt(DH * tokens)
    wide = queries.shape
    vmem = pl.BlockSpec(memory_space=pltpu.VMEM)
    hbm = pl.BlockSpec(memory_space=pltpu.HBM)
    pair = (DH, PAIR)
    held = pl.pallas_call(
        functools.partial(carry_kernel, factor, ny),
        out_shape=[
            jax.ShapeDtypeStruct(wide, BF16),
            jax.ShapeDtypeStruct(wide, BF16),
            jax.ShapeDtypeStruct(wide, F32),
            jax.ShapeDtypeStruct(wide, F32),
            jax.ShapeDtypeStruct(wide, BF16),
            jax.ShapeDtypeStruct(wide, BF16),
            jax.ShapeDtypeStruct((2,) + pair, BF16),
        ],
        in_specs=[hbm] * 4,
        out_specs=[vmem] * 7,
        scratch_shapes=[
            pltpu.VMEM(wide, BF16),
            pltpu.VMEM((BLOCK, PAIR), BF16),
            pltpu.VMEM((2, BLOCK, PAIR), BF16),
            pltpu.VMEM((2, BLOCK, PAIR), BF16),
            pltpu.VMEM((4, BLOCK, BLOCK), BF16),
            pltpu.VMEM(wide, F32),
            pltpu.VMEM(wide, F32),
            pltpu.VMEM((2, 2) + pair, F32),
            pltpu.VMEM((2,) + pair, F32),
            pltpu.VMEM((2,) + pair, F32),
            pltpu.VMEM((2,) + pair, BF16),
            pltpu.VMEM((QUAD - 1,) + pair, BF16),
            pltpu.VMEM((4,) + pair, F32),
            pltpu.VMEM(pair, BF16),
            pltpu.VMEM((QUADS - 1,) + pair, BF16),
            pltpu.VMEM((NZ,) + pair, BF16),
            pltpu.VMEM((2,) + pair, BF16),
            pltpu.VMEM((2, 2, NX) + pair, BF16),
            pltpu.VMEM((2,) + pair, F32),
            pltpu.VMEM((2,) + pair, F32),
            pltpu.VMEM((2, 2) + pair, F32),
            pltpu.SemaphoreType.DMA((5,)),
            pltpu.SemaphoreType.DMA((2 * ny,)),
            pltpu.SemaphoreType.DMA((2 * ny,)),
            pltpu.SemaphoreType.DMA((3,)),
            pltpu.SemaphoreType.DMA((3,)),
            pltpu.SemaphoreType.DMA((QUAD - 1,)),
            pltpu.SemaphoreType.DMA((QUAD - 1,)),
            pltpu.SemaphoreType.DMA((QUADS - 1,)),
            pltpu.SemaphoreType.DMA((QUADS - 1,)),
            pltpu.SemaphoreType.DMA((NZ,)),
            pltpu.SemaphoreType.DMA((NZ,)),
            pltpu.SemaphoreType.DMA((2, NX, 2)),
            pltpu.SemaphoreType.DMA((2, 2, NX)),
            pltpu.SemaphoreType.DMA((2,)),
            pltpu.SemaphoreType.DMA((2,)),
            pltpu.SemaphoreType.REGULAR((ROUNDS, 2)),
        ],
        compiler_params=pltpu.CompilerParams(
            collective_id=0, has_side_effects=True, vmem_limit_bytes=16 << 20
        ),
        name="carry",
    )(*[pltpu.with_memory_space_constraint(a, pltpu.HBM) for a in (queries, keys, values, out_grad)])
    return pl.pallas_call(
        functools.partial(finish_kernel, factor),
        out_shape=[jax.ShapeDtypeStruct(wide, BF16)] * 4,
        in_specs=[vmem] * 7,
        out_specs=[hbm] * 4,
        scratch_shapes=[
            pltpu.VMEM(wide, BF16),
            pltpu.VMEM(wide, BF16),
            pltpu.SemaphoreType.DMA((4,)),
        ],
        compiler_params=pltpu.CompilerParams(vmem_limit_bytes=16 << 20),
        name="finish",
    )(*held)


def solution(mesh):
    split = P("seq", "head")
    return jax.shard_map(
        on_device,
        mesh=mesh,
        in_specs=(split, split, split, P(("seq", "head"), None)),
        out_specs=(split, split, split, split),
        check_vma=False,
    )
```

time: 42.9 us -> 38.5 us (0.90)
  Pallas kernels: 42.1 us -> 37.8 us
    pallas_call x1, Pallas kernels: 41.2 us -> 36.8 us  [on_device(): pl.pallas_call(functools.partial(carry_kernel, factor, ny), out_shape=[ja...]
where the time goes in v2:
time: 38.5 us; the launch traced here: 38.4 us
  Pallas kernels  37.8 us (98%)
  between operations  0.64 us (2%)
    pallas_call x1, Pallas kernels, on_device(): pl.pallas_call(functools.partial(carry_kernel, factor, ny), out_shape=[ja...  36.8 us
    pallas_call x1, Pallas kernels, on_device(): pl.pallas_call(functools.partial(finish_kernel, factor), out_shape=[jax.S...  0.95 us

profile of v2, /device:TPU:1, one launch (start us, length us, event | category | flops | bytes accessed | tf_op | source)
XLA Modules:
  0.0 38.4 jit_solution(12747004557213402794)
XLA Ops:
  0.6 36.8 %carry.1 = (bf16[256,256]{1,0:T(8,128)(2,1)S(1)}, bf16[256,256]{1,0:T(8,128)(2,1)S(1)}, f32[256,256]{1,0:T(8,128)S(1)}, f32[256,256]{1,0:T(8,128)S(1)}, bf16[256...) custom-call(bf16[256,256]{1,0:T(8,128)(2,1)} %q_hbm.1, ...), custom_call_target="tpu_custom_call" | custom-call | tf_op jit(solution)/shard_map/carry/pallas_call | solution.py:371
  37.5 1.0 %finish.1 = (bf16[256,256]{1,0:T(8,128)(2,1)}, bf16[256,256]{1,0:T(8,128)(2,1)}, bf16[256,256]{1,0:T(8,128)(2,1)}, bf16[256,256]{1,0:T(8,128)(2,1)}) custom-call(bf16[256,256]{1,0:T(8,128)(2,1)S(1)} %get-tuple-element.11.att_in, bf16[256,256]{1,0:T(8,128)(2,1)S(1)} %get-tuple-element.12.qg_in, f32[256,256]{1,0:T(8,128)S(1)} %get-tuple-element.13.kg_part, ...), custom_call_target="tpu_custom_call" | custom-call | tf_op jit(solution)/shard_map/finish/pallas_call | solution.py:428

commit v3 on v2

--- a/solution.py
+++ b/solution.py
@@ -141,7 +141,7 @@
 
     sent = []
 
-    def send(src, dst, send_sem, recv_sem, to, when=None):
+    def send(src, dst, send_sem, recv_sem, to):
         copy = pltpu.make_async_remote_copy(
             src_ref=src,
             dst_ref=dst,
@@ -150,12 +150,21 @@
             device_id=(to, head),
             device_id_type=MESH,
         )
-        if when is None:
-            copy.start()
-        else:
-            pl.when(when)(copy.start)
-        sent.append((when, copy))
-        return copy
+        copy.start()
+        sent.append((None, [copy]))
+
+    def settle():
+        for when, copies in sent:
+            if when is None:
+                copies[0].wait_send()
+                continue
+
+            @pl.when(when)
+            def _():
+                for copy in copies:
+                    copy.wait_send()
+
+        sent.clear()
 
     def arrived(ref, sem):
         pltpu.make_async_copy(ref, ref, sem).wait()
@@ -211,45 +220,48 @@
             partial += masked((run - 1 - i) % QUADS < run, came)
         return whole, partial
 
+    turn_from = jnp.maximum(z - 2, 0)
+    others = [jnp.where(z == 0, 1, 0), jnp.where(z <= 1, 2, 1)]
+    others += [2 + (turn_from + i) % (NZ - 2) for i in range(1, NZ - 2)]
+
     def to_all():
         chip_sum(1)
-        for there in range(NZ):
-            send(
-                chip_out.at[1], z_in.at[z], z_send.at[there], z_recv.at[z], at(x, there, core),
-                jnp.logical_or(there < z, jnp.logical_and(there > z, x > 0)),
-            )
+        for i, there in enumerate(others):
+            send(chip_out.at[1], z_in.at[z], z_send.at[i], z_recv.at[z], at(x, there, core))
 
     def later():
-        whole_acc = sums.at[2]
-        part_acc = sums.at[3]
-        whole_acc[...] = chip[1]
-        part_acc[...] = jnp.zeros((DH, PAIR), F32)
-        for there in range(NZ):
-
-            @pl.when(there > z)
-            def _():
-                arrived(z_in.at[there], z_recv.at[there])
-                came = z_in[there].astype(F32)
-                whole_acc[...] += came
-                part_acc[...] += came
-
-            @pl.when(jnp.logical_and(there < z, x > 0))
-            def _():
-                arrived(z_in.at[there], z_recv.at[there])
-                whole_acc[...] += z_in[there].astype(F32)
-
-        return whole_acc[...], part_acc[...]
+        for there in others:
+            arrived(z_in.at[there], z_recv.at[there])
+        whole = chip[1]
+        partial = jnp.zeros((DH, PAIR), F32)
+        for there in others:
+            came = z_in[there].astype(F32)
+            whole += came
+            partial += masked(there > z, came)
+        return whole, partial
 
     def to_x(way):
         whole, partial = (earlier, later)[way]()
         x_out[way] = whole.astype(BF16)
-        for there in range(NX):
-            for c in range(2):
-                send(
-                    x_out.at[way], x_in.at[way, core, x],
-                    x_send.at[way, there, c], x_recv.at[way, core, x],
-                    at(there, z, c), before(way, x, there),
+        for there in range(1, NX) if way == 0 else range(NX - 1):
+            copies = [
+                pltpu.make_async_remote_copy(
+                    src_ref=x_out.at[way],
+                    dst_ref=x_in.at[way, core, x],
+                    send_sem=x_send.at[way, there, c],
+                    recv_sem=x_recv.at[way, core, x],
+                    device_id=(at(there, z, c), head),
+                    device_id_type=MESH,
                 )
+                for c in range(2)
+            ]
+
+            @pl.when(before(way, x, there))
+            def _():
+                for copy in copies:
+                    copy.start()
+
+            sent.append((before(way, x, there), copies))
         carries = core == 1 - way
         total[way, core] = partial + masked(carries, core_in[way])
         rest_out[way] = partial + masked(jnp.logical_not(carries), state[way, core])
@@ -258,7 +270,7 @@
     def finish(way):
         arrived(rest_in.at[way], rest_recv.at[way])
         total[way, 1 - core] = rest_in[way]
-        for there in range(NX):
+        for there in range(NX - 1) if way == 0 else range(1, NX):
 
             @pl.when(before(way, there, x))
             def _():
@@ -324,19 +336,15 @@
     backward_part()
 
     to_x(0)
+    sent.extend((None, [copy]) for copy in exchange)
+    settle()
     to_x(1)
     finish(0)
     for p in range(2):
         prefix = spread(total[0, p].astype(BF16))
         att[:, lanes[p]] = (att_part[:, lanes[p]] + factor * dot(q[:, lanes[p]], prefix)).astype(BF16)
         qg[:, lanes[p]] = (qg_part[:, lanes[p]] + factor * dot_t(g[p], prefix)).astype(BF16)
-    for copy in exchange:
-        copy.wait_send()
-    for when, copy in sent:
-        if when is None:
-            copy.wait_send()
-        else:
-            pl.when(when)(copy.wait_send)
+    settle()
     finish(1)
     suffix[...] = total[1].astype(BF16)
 

time: 38.5 us -> 38.4 us (level)
  no operation moved by 1% of the time
where the time goes in v3:
time: 38.4 us; the launch traced here: 38.2 us
  Pallas kernels  37.6 us (98%)
  between operations  0.64 us (2%)
    pallas_call x1, Pallas kernels, on_device(): pl.pallas_call(functools.partial(carry_kernel, factor, ny), out_shape=[ja...  36.6 us
    pallas_call x1, Pallas kernels, on_device(): pl.pallas_call(functools.partial(finish_kernel, factor), out_shape=[jax.S...  0.95 us

profile of v3, /device:TPU:1, one launch (start us, length us, event | category | flops | bytes accessed | tf_op | source)
XLA Modules:
  0.0 38.2 jit_solution(6137204383123449120)
XLA Ops:
  0.6 36.6 %carry.1 = (bf16[256,256]{1,0:T(8,128)(2,1)S(1)}, bf16[256,256]{1,0:T(8,128)(2,1)S(1)}, f32[256,256]{1,0:T(8,128)S(1)}, f32[256,256]{1,0:T(8,128)S(1)}, bf16[256...) custom-call(bf16[256,256]{1,0:T(8,128)(2,1)} %q_hbm.1, ...), custom_call_target="tpu_custom_call" | custom-call | tf_op jit(solution)/shard_map/carry/pallas_call | solution.py:379
  37.3 1.0 %finish.1 = (bf16[256,256]{1,0:T(8,128)(2,1)}, bf16[256,256]{1,0:T(8,128)(2,1)}, bf16[256,256]{1,0:T(8,128)(2,1)}, bf16[256,256]{1,0:T(8,128)(2,1)}) custom-call(bf16[256,256]{1,0:T(8,128)(2,1)S(1)} %get-tuple-element.11.att_in, bf16[256,256]{1,0:T(8,128)(2,1)S(1)} %get-tuple-element.12.qg_in, f32[256,256]{1,0:T(8,128)S(1)} %get-tuple-element.13.kg_part, ...), custom_call_target="tpu_custom_call" | custom-call | tf_op jit(solution)/shard_map/finish/pallas_call | solution.py:436

commit v4 on v3

--- a/solution.py
+++ b/solution.py
@@ -141,7 +141,7 @@
 
     sent = []
 
-    def send(src, dst, send_sem, recv_sem, to):
+    def send(src, dst, send_sem, recv_sem, to, when=None):
         copy = pltpu.make_async_remote_copy(
             src_ref=src,
             dst_ref=dst,
@@ -150,8 +150,11 @@
             device_id=(to, head),
             device_id_type=MESH,
         )
-        copy.start()
-        sent.append((None, [copy]))
+        if when is None:
+            copy.start()
+        else:
+            pl.when(when)(copy.start)
+        sent.append((when, [copy]))
 
     def settle():
         for when, copies in sent:
@@ -227,15 +230,18 @@
     def to_all():
         chip_sum(1)
         for i, there in enumerate(others):
-            send(chip_out.at[1], z_in.at[z], z_send.at[i], z_recv.at[z], at(x, there, core))
+            send(chip_out.at[1], z_in.at[z], z_send.at[i], z_recv.at[z], at(x, there, core),
+                jnp.logical_or(there < z, x > 0))
 
     def later():
         for there in others:
-            arrived(z_in.at[there], z_recv.at[there])
+            pl.when(jnp.logical_or(there > z, x > 0))(
+                functools.partial(arrived, z_in.at[there], z_recv.at[there])
+            )
         whole = chip[1]
         partial = jnp.zeros((DH, PAIR), F32)
         for there in others:
-            came = z_in[there].astype(F32)
+            came = masked(jnp.logical_or(there > z, x > 0), z_in[there].astype(F32))
             whole += came
             partial += masked(there > z, came)
         return whole, partial

time: 38.4 us -> 38.4 us (level)
  no operation moved by 1% of the time
where the time goes in v4:
time: 38.4 us; the launch traced here: 38.3 us
  Pallas kernels  37.6 us (98%)
  between operations  0.64 us (2%)
    pallas_call x1, Pallas kernels, on_device(): pl.pallas_call(functools.partial(carry_kernel, factor, ny), out_shape=[ja...  36.7 us
    pallas_call x1, Pallas kernels, on_device(): pl.pallas_call(functools.partial(finish_kernel, factor), out_shape=[jax.S...  0.95 us

profile of v4, /device:TPU:1, one launch (start us, length us, event | category | flops | bytes accessed | tf_op | source)
XLA Modules:
  0.0 38.3 jit_solution(16417346083792608751)
XLA Ops:
  0.6 36.7 %carry.1 = (bf16[256,256]{1,0:T(8,128)(2,1)S(1)}, bf16[256,256]{1,0:T(8,128)(2,1)S(1)}, f32[256,256]{1,0:T(8,128)S(1)}, f32[256,256]{1,0:T(8,128)S(1)}, bf16[256...) custom-call(bf16[256,256]{1,0:T(8,128)(2,1)} %q_hbm.1, ...), custom_call_target="tpu_custom_call" | custom-call | tf_op jit(solution)/shard_map/carry/pallas_call | solution.py:385
  37.3 1.0 %finish.1 = (bf16[256,256]{1,0:T(8,128)(2,1)}, bf16[256,256]{1,0:T(8,128)(2,1)}, bf16[256,256]{1,0:T(8,128)(2,1)}, bf16[256,256]{1,0:T(8,128)(2,1)}) custom-call(bf16[256,256]{1,0:T(8,128)(2,1)S(1)} %get-tuple-element.11.att_in, bf16[256,256]{1,0:T(8,128)(2,1)S(1)} %get-tuple-element.12.qg_in, f32[256,256]{1,0:T(8,128)S(1)} %get-tuple-element.13.kg_part, ...), custom_call_target="tpu_custom_call" | custom-call | tf_op jit(solution)/shard_map/finish/pallas_call | solution.py:442
